TPU v7x, 256 devices: a whole 4x4x8 slice. The times are simulated.
256 devices in a mesh: dp: 32 (over y, z), tensor: 8 (over x, core).
Axes of the slice: x: 4, y: 4, z: 8, core: 2. Of those that a mesh axis runs over, the one named last changes fastest.
Arguments:
- queries: bfloat16 [256, 6, 8192], P('dp', None, 'tensor'), may hold values from -150 to 150
- new_keys: bfloat16 [256, 6, 1024], P('dp', None, 'tensor'), may hold values from -6 to 6
- new_values: bfloat16 [256, 6, 1024], P('dp', None, 'tensor'), may hold values from -6 to 6
- key_cache: bfloat16 [256, 256, 1024], P('dp', None, 'tensor'), may hold values from -6 to 6
- value_cache: bfloat16 [256, 256, 1024], P('dp', None, 'tensor'), may hold values from -6 to 6
- cache_lengths: int32 [256], P('dp'), may hold values from 32 to 256, as said below
- accepted: int32 [256], P('tensor'), may hold values from 1 to 6
- residual: bfloat16 [256, 6, 8192], P('tensor', None, 'dp'), may hold values from -6 to 6
- out_weight: bfloat16 [8192, 8192], P('tensor', 'dp'), may hold values from -0.0625 to 0.0625
- draft_weight: bfloat16 [8192, 8192], P('tensor', 'dp'), may hold values from -0.0625 to 0.0625
Outputs:
- verified: bfloat16 [256, 6, 8192], P('tensor', None, 'dp')
- drafted: bfloat16 [5, 256, 8192], P(None, 'tensor', 'dp')
Inputs may be any that keep to these rules, and one draw needn't show every extreme that they name: `cache_lengths`: every draw has a window with all 256 slots live.
All inputs are finite; a program needn't handle non-finite values.
Results may differ from a plain program's by a relative error of at most 0.008.
Values may be sent and summed in bfloat16 or wider, within the bound.
No kernel may reach another device: no remote copies, remote signals or barrier semaphores. Data moves between devices by JAX's collectives and lax.ppermute only.
A program may use at most 64 MiB of HBM per device.

v0:
```python
import jax
import jax.numpy as jnp
from jax import lax
from jax.sharding import PartitionSpec as P

HD = 128
STEPS = 5


def spread(block, axis):
    copies = jnp.broadcast_to(block[None], (lax.axis_size(axis),) + block.shape)
    return lax.all_to_all(copies, axis, split_axis=0, concat_axis=0, tiled=True)


def accepted_of_my_windows(accepted):
    dp_size, tensor_size = (lax.axis_size("dp"), lax.axis_size("tensor"))
    ratio = dp_size // tensor_size
    pairs = []
    for j in range(dp_size):
        for i in range(tensor_size):
            source = (ratio * i + j % ratio) * tensor_size + j // ratio
            pairs.append((source, j * tensor_size + i))
    block = lax.ppermute(accepted, ("dp", "tensor"), pairs)
    rows = accepted.shape[0] // ratio
    return lax.dynamic_slice_in_dim(block, lax.axis_index("dp") % ratio * rows, rows, 0)


def pick(rows, accepted):
    chosen = jnp.arange(rows.shape[1])[None, :] == (accepted - 1)[:, None]
    return jnp.sum(
        jnp.where(chosen[:, :, None], rows, jnp.zeros((), rows.dtype)), axis=1, dtype=rows.dtype
    )


def per_device(
    queries,
    new_keys,
    new_values,
    key_cache,
    value_cache,
    cache_lengths,
    accepted,
    residual,
    out_weight,
    draft_weight,
):
    windows_here, tokens_here, query_width = queries.shape
    cache_size = key_cache.shape[1]
    kv_here = new_keys.shape[2] // HD
    group_size = query_width // HD // kv_here
    tensor_size = lax.axis_size("tensor")
    own_accepted = accepted_of_my_windows(accepted)
    draft_columns = lax.all_gather(draft_weight, "tensor", axis=0, tiled=True)
    query_split = queries.reshape(windows_here, tokens_here, kv_here, group_size, HD)
    keys_cached = key_cache.reshape(windows_here, cache_size, kv_here, HD)
    keys_fresh = new_keys.reshape(windows_here, tokens_here, kv_here, HD)
    score_cache = jnp.einsum(
        "wtkgd,wpkd->wkgtp", query_split, keys_cached, preferred_element_type=jnp.float32
    ) * HD ** (-0.5)
    score_fresh = jnp.einsum(
        "wtkgd,wpkd->wkgtp", query_split, keys_fresh, preferred_element_type=jnp.float32
    ) * HD ** (-0.5)
    live_cache = (jnp.arange(cache_size)[None, :] < cache_lengths[:, None])[:, None, None, None, :]
    live_fresh = jnp.arange(tokens_here)[None, :] <= jnp.arange(tokens_here)[:, None]
    scores = jnp.concatenate(
        [
            jnp.where(live_cache, score_cache, -jnp.inf),
            jnp.where(live_fresh, score_fresh, -jnp.inf),
        ],
        axis=-1,
    )
    largest = jnp.max(scores, axis=-1, keepdims=True)
    powered = jnp.exp(scores - largest)
    weights = (powered / jnp.sum(powered, axis=-1, keepdims=True)).astype(jnp.bfloat16)
    values_cached = value_cache.reshape(windows_here, cache_size, kv_here, HD)
    values_fresh = new_values.reshape(windows_here, tokens_here, kv_here, HD)
    mixed_rows = jnp.einsum(
        "wkgtp,wpkd->wtkgd",
        weights[..., :cache_size],
        values_cached,
        preferred_element_type=jnp.float32,
    )
    mixed_rows = mixed_rows + jnp.einsum(
        "wkgtp,wpkd->wtkgd",
        weights[..., cache_size:],
        values_fresh,
        preferred_element_type=jnp.float32,
    )
    attended = mixed_rows.astype(jnp.bfloat16).reshape(windows_here, tokens_here, query_width)
    picked_rows = spread(pick(attended, own_accepted), "dp").reshape(-1, query_width)
    picked_part = jnp.dot(picked_rows, out_weight, preferred_element_type=jnp.float32)
    block_windows, block_tokens, block_cols = residual.shape
    shares = lax.all_to_all(
        picked_part.astype(jnp.bfloat16).reshape(tensor_size, block_windows, block_cols),
        "tensor",
        split_axis=0,
        concat_axis=0,
        tiled=True,
    )
    current = (
        pick(residual, accepted).astype(jnp.float32) + jnp.sum(shares.astype(jnp.float32), axis=0)
    ).astype(jnp.bfloat16)
    partial_out = jnp.dot(
        lax.all_gather(
            attended.reshape(windows_here * tokens_here, query_width), "dp", axis=0, tiled=True
        ),
        out_weight,
        preferred_element_type=jnp.float32,
    )
    summed = lax.psum_scatter(partial_out, "tensor", scatter_dimension=0, tiled=True)
    flat_residual = residual.reshape(block_windows * block_tokens, block_cols).astype(jnp.float32)
    verified = (
        (flat_residual + summed)
        .astype(jnp.bfloat16)
        .reshape(block_windows, block_tokens, block_cols)
    )
    columns = draft_columns.reshape(-1, block_cols, draft_columns.shape[1])
    results = []
    for draft_step in range(STEPS):
        inputs = spread(current, "dp")
        product = jnp.einsum("jwk,jkn->wn", inputs, columns, preferred_element_type=jnp.float32)
        current = jnp.tanh(2.0 * product).astype(jnp.bfloat16)
        results.append(current)
    return (verified, jnp.stack(results))


def solution(mesh):
    placed = (
        P("dp", None, "tensor"),
        P("dp", None, "tensor"),
        P("dp", None, "tensor"),
        P("dp", None, "tensor"),
        P("dp", None, "tensor"),
        P("dp"),
        P("tensor"),
        P("tensor", None, "dp"),
        P("tensor", "dp"),
        P("tensor", "dp"),
    )
    return jax.shard_map(
        per_device,
        mesh=mesh,
        in_specs=placed,
        out_specs=(P("tensor", None, "dp"), P(None, "tensor", "dp")),
        check_vma=False,
    )
```

profile of v0, /device:TPU:32, one launch (start us, length us, event | category | flops | bytes accessed | tf_op | source)
XLA Modules:
  0.0 202.9 jit_solution(7244637274583813440)
XLA Ops:
  8.0 1.3 collective-permute-start
  10.0 1.2 fusion.35
  11.2 1.4 fusion.34
  14.1 1.3 fusion.29
  16.1 0.9 broadcast_in_dim.104
  16.9 19.1 %all-to-all-start = ((bf16[32,8,1024]{2,1,0:T(8,128)(2,1)}), bf16[32,8,1024]{2,1,0:T(8,128)(2,1)S(1)}, u32[]{:S(2)}, u32[]{:S(2)}) async-start(bf16[32,8,1024]{2,1,0:T(8,128)(2,1)} %broadcast_in_dim.104), calls=%async_computation.1 | async-start | bytes 1048576 | tf_op jit(solution)/shard_map/all_to_all | solution.py:12
  36.1 15.0 %all-to-all-done = bf16[32,8,1024]{2,1,0:T(8,128)(2,1)S(1)} async-done(((bf16[32,8,1024]{2,1,0:T(8,128)(2,1)}), bf16[32,8,1024]{2,1,0:T(8,128)(2,1)S(1)}, u32[]{:S(2)}, u32[]{:S(2)}) %all-to-all-start) | async-done | bytes 524320 | tf_op jit(solution)/shard_map/all_to_all | solution.py:12
  51.1 1.0 convolution_convert_fusion
  52.0 3.4 %all-to-all-start.1 = ((bf16[8,32,256]{2,1,0:T(8,128)(2,1)}), bf16[8,32,256]{2,1,0:T(8,128)(2,1)S(1)}, u32[]{:S(2)}, u32[]{:S(2)}) async-start(bf16[8,32,256]{2,1,0:T(8,128)(2,1)} %bitcast.19), calls=%async_computation.2 | async-start | bytes 262144 | tf_op jit(solution)/shard_map/all_to_all | solution.py:93
  55.5 5.9 %all-to-all-done.1 = bf16[8,32,256]{2,1,0:T(8,128)(2,1)S(1)} async-done(((bf16[8,32,256]{2,1,0:T(8,128)(2,1)}), bf16[8,32,256]{2,1,0:T(8,128)(2,1)S(1)}, u32[]{:S(2)}, u32[]{:S(2)}) %all-to-all-start.1) | async-done | bytes 131104 | tf_op jit(solution)/shard_map/all_to_all | solution.py:93
  61.6 23.8 %all_to_all.35 = bf16[32,32,256]{2,1,0:T(8,128)(2,1)S(1)} all-to-all(bf16[32,32,256]{2,1,0:T(8,128)(2,1)S(1)} %broadcast_in_dim.105), channel_id=1, replica_groups=mesh['dp'=32,'tensor'=8] {'dp'}, dimensions={0} | all-to-all | bytes 1048576 | tf_op jit(solution)/shard_map/all_to_all | solution.py:12
  85.4 3.2 %bitcast_dynamic-update-slice_fusion.3 = (bf16[5,32,256]{2,1,0:T(8,128)(2,1)S(1)}, bf16[32,256]{1,0:T(8,128)(2,1)S(1)}) fusion(bf16[32,32,256]{2,1,0:T(8,128)(2,1)S(1)} %all_to_all.35, bf16[32,256,256]{2,1,0:T(8,128)(2,1)} %bitcast.131), kind=kOutput, calls=%fused_computation.55 | convolution fusion | flops 134234112 | bytes 4751360 | tf_op jit(solution)/shard_map/jwk,jkn->wn/dot_general | solution.py:121
  88.6 23.2 %all_to_all.36 = bf16[32,32,256]{2,1,0:T(8,128)(2,1)S(1)} all-to-all(bf16[32,32,256]{2,1,0:T(8,128)(2,1)S(1)} %broadcast_in_dim.106), channel_id=1, replica_groups=mesh['dp'=32,'tensor'=8] {'dp'}, dimensions={0} | all-to-all | bytes 1048576 | tf_op jit(solution)/shard_map/all_to_all | solution.py:12
  112.7 0.9 broadcast_in_dim.107
  113.6 5.5 %all-to-all-start.4 = ((bf16[32,32,256]{2,1,0:T(8,128)(2,1)}), bf16[32,32,256]{2,1,0:T(8,128)(2,1)S(1)}, u32[]{:S(2)}, u32[]{:S(2)}) async-start(bf16[32,32,256]{2,1,0:T(8,128)(2,1)} %broadcast_in_dim.107), calls=%async_computation.5 | async-start | bytes 1048576 | tf_op jit(solution)/shard_map/all_to_all | solution.py:12
  119.2 18.9 %all-gather.3.cloned.1.call-done = bf16[1536,1024]{1,0:T(8,128)(2,1)} async-done(((bf16[48,1024]{1,0:T(8,128)(2,1)}), bf16[1536,1024]{1,0:T(8,128)(2,1)}) %all-gather.3.cloned.1.call-update) | async-done | bytes 3145744 | tf_op jit(solution)/shard_map/all_gather | solution.py:104
  138.1 4.1 %fusion.36 = f32[1536,256]{1,0:T(8,128)} fusion(bf16[1536,1024]{1,0:T(8,128)(2,1)} %all-gather.3.cloned.1.call-done, bf16[1024,256]{1,0:T(8,128)(2,1)S(1)} %copy-done), kind=kOutput, calls=%fused_computation.66 | convolution fusion | flops 805306368 | bytes 5242880 | tf_op jit(solution)/shard_map/dot_general | solution.py:103
  142.2 3.2 %bitcast_dynamic-update-slice_fusion.1 = (bf16[5,32,256]{2,1,0:T(8,128)(2,1)S(1)}, bf16[32,256]{1,0:T(8,128)(2,1)S(1)}) fusion(bf16[5,32,256]{2,1,0:T(8,128)(2,1)S(1)} %get-tuple-element.14, bf16[32,32,256]{2,1,0:T(8,128)(2,1)S(1)} %all-to-all-done.4, bf16[32,256,256]{2,1,0:T(8,128)(2,1)} %bitcast.132), kind=kOutput, calls=%fused_computation.53 | convolution fusion | flops 134234112 | bytes 4751360 | tf_op jit(solution)/shard_map/jwk,jkn->wn/dot_general | solution.py:121
  145.5 24.1 %all_to_all.37 = bf16[32,32,256]{2,1,0:T(8,128)(2,1)S(1)} all-to-all(bf16[32,32,256]{2,1,0:T(8,128)(2,1)S(1)} %broadcast_in_dim.108), channel_id=1, replica_groups=mesh['dp'=32,'tensor'=8] {'dp'}, dimensions={0} | all-to-all | bytes 1048576 | tf_op jit(solution)/shard_map/all_to_all | solution.py:12
  170.4 0.9 broadcast_in_dim.109
  171.3 4.8 %all-to-all-start.6 = ((bf16[32,32,256]{2,1,0:T(8,128)(2,1)}), bf16[32,32,256]{2,1,0:T(8,128)(2,1)S(1)}, u32[]{:S(2)}, u32[]{:S(2)}) async-start(bf16[32,32,256]{2,1,0:T(8,128)(2,1)} %broadcast_in_dim.109), calls=%async_computation.7 | async-start | bytes 1048576 | tf_op jit(solution)/shard_map/all_to_all | solution.py:12
  176.5 0.9 add_convert_fusion
  178.1 14.5 %all-to-all-done.6 = bf16[32,32,256]{2,1,0:T(8,128)(2,1)S(1)} async-done(((bf16[32,32,256]{2,1,0:T(8,128)(2,1)}), bf16[32,32,256]{2,1,0:T(8,128)(2,1)S(1)}, u32[]{:S(2)}, u32[]{:S(2)}) %all-to-all-start.6) | async-done | bytes 524320 | tf_op jit(solution)/shard_map/all_to_all | solution.py:12
  192.7 3.0 %fusion.22 = bf16[5,32,256]{2,1,0:T(8,128)(2,1)S(1)} fusion(bf16[5,32,256]{2,1,0:T(8,128)(2,1)S(1)} %get-tuple-element.18, bf16[32,32,256]{2,1,0:T(8,128)(2,1)S(1)} %all-to-all-done.6, bf16[32,256,256]{2,1,0:T(8,128)(2,1)} %bitcast.133), kind=kOutput, calls=%fused_computation.31 | convolution fusion | flops 134234112 | bytes 4734976 | tf_op jit(solution)/shard_map/jwk,jkn->wn/dot_general | solution.py:121
  (46 shorter events, 7.3 us)
Async XLA Ops:
  7.2 43.9 %copy-start = (bf16[1024,256]{1,0:T(8,128)(2,1)S(1)}, bf16[1024,256]{1,0:T(8,128)(2,1)}, u32[]{:S(2)}) copy-start(bf16[1024,256]{1,0:T(8,128)(2,1)} %param.18) | copy-start | bytes 1572868
  7.2 28.9 %copy-start.5 = (s32[32]{0:T(128)S(1)}, s32[32]{0:T(128)}, u32[]{:S(2)}) copy-start(s32[32]{0:T(128)} %param.16) | copy-start | bytes 388
  7.2 48.2 %copy-start.3 = (bf16[32,6,256]{2,0,1:T(8,128)(2,1)S(1)}, bf16[32,6,256]{2,0,1:T(8,128)(2,1)}, u32[]{:S(2)}) copy-start(bf16[32,6,256]{2,0,1:T(8,128)(2,1)} %param.17) | copy-start | bytes 294916
  7.2 78.2 %all-gather.5.cloned.1.call-start = ((), (), s32[]{:S(2)}) async-start(), calls=%async_computation.10 | async-start | bytes 4718592 | tf_op jit(solution)/shard_map/all_gather | solution.py:53
  7.9 130.1 %all-gather.3.cloned.1.call-start = ((), (), s32[]{:S(2)}) async-start(), calls=%async_computation.8 | async-start | bytes 3244032 | tf_op jit(solution)/shard_map/all_gather | solution.py:104
  8.0 6.0 %collective-permute-start = (s32[32]{0:T(128)}, s32[32]{0:T(128)S(1)}, u32[]{:S(2)}, u32[]{:S(2)}) collective-permute-start(s32[32]{0:T(128)} %param.16), channel_id=1, source_target_pairs={{0,0},{32,1},{64,2},{96,3},{128,4},{160,5},{192,6},{224,7},{8,8},{... | collective-permute-start | bytes 392 | tf_op jit(solution)/shard_map/ppermute | solution.py:23
  16.9 34.2 %all-to-all-start = ((bf16[32,8,1024]{2,1,0:T(8,128)(2,1)}), bf16[32,8,1024]{2,1,0:T(8,128)(2,1)S(1)}, u32[]{:S(2)}, u32[]{:S(2)}) async-start(bf16[32,8,1024]{2,1,0:T(8,128)(2,1)} %broadcast_in_dim.104), calls=%async_computation.1 | async-start | bytes 1048576 | tf_op jit(solution)/shard_map/all_to_all | solution.py:12
  52.0 9.4 %all-to-all-start.1 = ((bf16[8,32,256]{2,1,0:T(8,128)(2,1)}), bf16[8,32,256]{2,1,0:T(8,128)(2,1)S(1)}, u32[]{:S(2)}, u32[]{:S(2)}) async-start(bf16[8,32,256]{2,1,0:T(8,128)(2,1)} %bitcast.19), calls=%async_computation.2 | async-start | bytes 262144 | tf_op jit(solution)/shard_map/all_to_all | solution.py:93
  85.4 26.5 %copy-start.1 = (bf16[8192,256]{1,0:T(8,128)(2,1)S(1)}, bf16[8192,256]{1,0:T(8,128)(2,1)}, u32[]{:S(2)}) copy-start(bf16[8192,256]{1,0:T(8,128)(2,1)} %all-gather.5.cloned.1.call-done) | copy-start | bytes 12582916
  113.6 28.6 %all-to-all-start.4 = ((bf16[32,32,256]{2,1,0:T(8,128)(2,1)}), bf16[32,32,256]{2,1,0:T(8,128)(2,1)S(1)}, u32[]{:S(2)}, u32[]{:S(2)}) async-start(bf16[32,32,256]{2,1,0:T(8,128)(2,1)} %broadcast_in_dim.107), calls=%async_computation.5 | async-start | bytes 1048576 | tf_op jit(solution)/shard_map/all_to_all | solution.py:12
  119.1 57.4 %reduce-scatter.2.cloned.1.call-start = ((), (), s32[]{:S(2)}) async-start(), calls=%async_computation.9 | async-start | bytes 1769472 | tf_op jit(solution)/shard_map/reduce_scatter | solution.py:110
  142.2 27.4 %copy-start.2 = (bf16[8192,256]{1,0:T(8,128)(2,1)S(1)}, bf16[8192,256]{1,0:T(8,128)(2,1)}, u32[]{:S(2)}) copy-start(bf16[8192,256]{1,0:T(8,128)(2,1)} %all-gather.5.cloned.1.call-done) | copy-start | bytes 12582916
  171.3 21.4 %all-to-all-start.6 = ((bf16[32,32,256]{2,1,0:T(8,128)(2,1)}), bf16[32,32,256]{2,1,0:T(8,128)(2,1)S(1)}, u32[]{:S(2)}, u32[]{:S(2)}) async-start(bf16[32,32,256]{2,1,0:T(8,128)(2,1)} %broadcast_in_dim.109), calls=%async_computation.7 | async-start | bytes 1048576 | tf_op jit(solution)/shard_map/all_to_all | solution.py:12
  195.7 0.6 copy-start.4
Sparse Core Ops, SparseCore 0:
  9.9 37.2 all-gather.4
  50.4 87.6 all-gather.2
  142.3 34.1 reduce-scatter.1
where the time goes:
time: 204 us; the launch traced here: 203 us
  blocking collectives  71.2 us (35%)
  waiting for transfers between devices  55.3 us (27%)
  starting transfers between devices  34.3 us (17%)
  matrix products  20.8 us (10%)
  between operations  14 us (7%)
  local copies, waits for them, and re-layouts  4.89 us (2%)
  other arithmetic  2.43 us (1%)
    all_to_all x3, blocking collectives, spread(): return lax.all_to_all(copies, axis, split_axis=0, concat_axis=0, tiled=True)  71.2 us
    all_to_all x3, waiting for transfers between devices, spread(): return lax.all_to_all(copies, axis, split_axis=0, concat_axis=0, tiled=True)  29.5 us
    all_to_all x3, starting transfers between devices, spread(): return lax.all_to_all(copies, axis, split_axis=0, concat_axis=0, tiled=True)  29.5 us
    all_gather x1, waiting for transfers between devices, per_device(): lax.all_gather(attended.reshape(windows_here * tokens_here, query_width),...  18.9 us
    dot_general x5, matrix products, per_device(): jnp.einsum('jwk,jkn->wn', inputs, columns, preferred_element_type=jnp.flo...  11 us
    all_to_all x1, waiting for transfers between devices, per_device(): lax.all_to_all(picked_part.astype(jnp.bfloat16).reshape(tensor_size, bloc...  5.94 us
    dot_general x1, matrix products, per_device(): jnp.dot(lax.all_gather(attended.reshape(windows_here * tokens_here, query...  4.12 us
  transfers between devices with their start and end apart: 8, of which 5 were waited for; matrix products, arithmetic and copies ran while one was open for 12% of the time, Pallas kernels for 0%

commit v1 on v0

--- a/solution.py
+++ b/solution.py
@@ -101,8 +101,17 @@
         pick(residual, accepted).astype(jnp.float32) + jnp.sum(shares.astype(jnp.float32), axis=0)
     ).astype(jnp.bfloat16)
     partial_out = jnp.dot(
-        lax.all_gather(
-            attended.reshape(windows_here * tokens_here, query_width), "dp", axis=0, tiled=True
+        jnp.concatenate(
+            lax.all_to_all(
+                jnp.stack(
+                    [attended.reshape(windows_here * tokens_here, query_width)]
+                    * lax.axis_size("dp")
+                ),
+                "dp",
+                0,
+                0,
+            ),
+            axis=0,
         ),
         out_weight,
         preferred_element_type=jnp.float32,

time: 204 us -> 272 us (1.33)
  waiting for transfers between devices: 55.3 us -> 134 us
  blocking collectives: 71.2 us -> 43.6 us
  starting transfers between devices: 34.3 us -> 46.5 us
    all_to_all x0 -> x1, waiting for transfers between devices: none -> 67.1 us  [per_device(): lax.all_to_all(jnp.stack([attended.reshape(windows_here * tokens_here, qu...]
    all_to_all x3 -> x4, waiting for transfers between devices: 29.5 us -> 60.1 us  [spread(): return lax.all_to_all(copies, axis, split_axis=0, concat_axis=0, tiled=True)]
    all_to_all x3 -> x2, blocking collectives: 71.2 us -> 43.6 us  [spread(): return lax.all_to_all(copies, axis, split_axis=0, concat_axis=0, tiled=True)]
    all_gather x1 -> x0, waiting for transfers between devices: 18.9 us -> none  [per_device(): lax.all_gather(attended.reshape(windows_here * tokens_here, query_width),...]
    all_to_all x3 -> x4, starting transfers between devices: 29.5 us -> 36.8 us  [spread(): return lax.all_to_all(copies, axis, split_axis=0, concat_axis=0, tiled=True)]
    all_to_all x0 -> x1, starting transfers between devices: none -> 4.91 us  [per_device(): lax.all_to_all(jnp.stack([attended.reshape(windows_here * tokens_here, qu...]
  transfers between devices with their start and end apart: 8 -> 9, of which waited for: 5 -> 6; matrix products, arithmetic and copies ran while one was open for 12% -> 8% of each run, Pallas kernels for 0% -> 0%
where the time goes in v1:
time: 272 us; the launch traced here: 271 us
  waiting for transfers between devices  134 us (49%)
  starting transfers between devices  46.5 us (17%)
  blocking collectives  43.6 us (16%)
  matrix products  22.8 us (8%)
  between operations  14.3 us (5%)
  local copies, waits for them, and re-layouts  7.17 us (3%)
    all_to_all x1, waiting for transfers between devices, per_device(): lax.all_to_all(jnp.stack([attended.reshape(windows_here * tokens_here, qu...  67.1 us
    all_to_all x4, waiting for transfers between devices, spread(): return lax.all_to_all(copies, axis, split_axis=0, concat_axis=0, tiled=True)  60.1 us
    all_to_all x2, blocking collectives, spread(): return lax.all_to_all(copies, axis, split_axis=0, concat_axis=0, tiled=True)  43.6 us
    all_to_all x4, starting transfers between devices, spread(): return lax.all_to_all(copies, axis, split_axis=0, concat_axis=0, tiled=True)  36.8 us
    dot_general x5, matrix products, per_device(): jnp.einsum('jwk,jkn->wn', inputs, columns, preferred_element_type=jnp.flo...  13.1 us
    all_to_all x1, waiting for transfers between devices, per_device(): lax.all_to_all(picked_part.astype(jnp.bfloat16).reshape(tensor_size, bloc...  5.94 us
  transfers between devices with their start and end apart: 9, of which 6 were waited for; matrix products, arithmetic and copies ran while one was open for 8% of the time, Pallas kernels for 0%

profile of v1, /device:TPU:32, one launch (start us, length us, event | category | flops | bytes accessed | tf_op | source)
XLA Modules:
  0.0 270.8 jit_solution(97152685743779370)
XLA Ops:
  7.9 1.3 collective-permute-start
  10.0 1.2 fusion.35
  11.1 1.4 fusion.34
  14.1 1.3 fusion.29
  16.2 19.1 %all-to-all-start.1 = ((bf16[32,8,1024]{2,1,0:T(8,128)(2,1)}), bf16[32,8,1024]{2,1,0:T(8,128)(2,1)S(1)}, u32[]{:S(2)}, u32[]{:S(2)}) async-start(bf16[32,8,1024]{2,1,0:T(8,128)(2,1)} %broadcast_in_dim.104), calls=%async_computation.2 | async-start | bytes 1048576 | tf_op jit(solution)/shard_map/all_to_all | solution.py:12
  35.4 15.0 %all-to-all-done.1 = bf16[32,8,1024]{2,1,0:T(8,128)(2,1)S(1)} async-done(((bf16[32,8,1024]{2,1,0:T(8,128)(2,1)}), bf16[32,8,1024]{2,1,0:T(8,128)(2,1)S(1)}, u32[]{:S(2)}, u32[]{:S(2)}) %all-to-all-start.1) | async-done | bytes 524320 | tf_op jit(solution)/shard_map/all_to_all | solution.py:12
  51.3 3.4 %all-to-all-start.2 = ((bf16[8,32,256]{2,1,0:T(8,128)(2,1)}), bf16[8,32,256]{2,1,0:T(8,128)(2,1)S(1)}, u32[]{:S(2)}, u32[]{:S(2)}) async-start(bf16[8,32,256]{2,1,0:T(8,128)(2,1)} %bitcast.20), calls=%async_computation.3 | async-start | bytes 262144 | tf_op jit(solution)/shard_map/all_to_all | solution.py:93
  54.8 5.9 %all-to-all-done.2 = bf16[8,32,256]{2,1,0:T(8,128)(2,1)S(1)} async-done(((bf16[8,32,256]{2,1,0:T(8,128)(2,1)}), bf16[8,32,256]{2,1,0:T(8,128)(2,1)S(1)}, u32[]{:S(2)}, u32[]{:S(2)}) %all-to-all-start.2) | async-done | bytes 131104 | tf_op jit(solution)/shard_map/all_to_all | solution.py:93
  60.8 22.1 %all_to_all.40 = bf16[32,32,256]{2,1,0:T(8,128)(2,1)S(1)} all-to-all(bf16[32,32,256]{2,1,0:T(8,128)(2,1)S(1)} %broadcast_in_dim.105), channel_id=1, replica_groups=mesh['dp'=32,'tensor'=8] {'dp'}, dimensions={0} | all-to-all | bytes 1048576 | tf_op jit(solution)/shard_map/all_to_all | solution.py:12
  82.9 3.0 %bitcast_dynamic-update-slice_fusion.3 = (bf16[5,32,256]{2,1,0:T(8,128)(2,1)S(1)}, bf16[32,256]{1,0:T(8,128)(2,1)S(1)}) fusion(bf16[32,32,256]{2,1,0:T(8,128)(2,1)S(1)} %all_to_all.40, bf16[32,256,256]{2,1,0:T(8,128)(2,1)} %bitcast.132), kind=kOutput, calls=%fused_computation.55 | convolution fusion | flops 134234112 | bytes 4751360 | tf_op jit(solution)/shard_map/jwk,jkn->wn/dot_general | solution.py:130
  86.8 4.8 %all-to-all-start.4 = ((bf16[32,32,256]{2,1,0:T(8,128)(2,1)}), bf16[32,32,256]{2,1,0:T(8,128)(2,1)S(1)}, u32[]{:S(2)}, u32[]{:S(2)}) async-start(bf16[32,32,256]{2,1,0:T(8,128)(2,1)} %broadcast_in_dim.106), calls=%async_computation.5 | async-start | bytes 1048576 | tf_op jit(solution)/shard_map/all_to_all | solution.py:12
  91.7 16.9 %all-to-all-done.4 = bf16[32,32,256]{2,1,0:T(8,128)(2,1)S(1)} async-done(((bf16[32,32,256]{2,1,0:T(8,128)(2,1)}), bf16[32,32,256]{2,1,0:T(8,128)(2,1)S(1)}, u32[]{:S(2)}, u32[]{:S(2)}) %all-to-all-start.4) | async-done | bytes 524320 | tf_op jit(solution)/shard_map/all_to_all | solution.py:12
  108.6 2.1 stack.21
  110.7 4.9 %all-to-all-start = ((bf16[32,48,1024]{2,1,0:T(8,128)(2,1)}), bf16[32,48,1024]{2,1,0:T(8,128)(2,1)}, u32[]{:S(2)}, u32[]{:S(2)}) async-start(bf16[32,48,1024]{2,1,0:T(8,128)(2,1)} %stack.21), calls=%async_computation | async-start | bytes 6291456 | tf_op jit(solution)/shard_map/all_to_all | solution.py:105
  115.6 3.0 %bitcast_dynamic-update-slice_fusion.2 = (bf16[5,32,256]{2,1,0:T(8,128)(2,1)S(1)}, bf16[32,256]{1,0:T(8,128)(2,1)S(1)}) fusion(bf16[5,32,256]{2,1,0:T(8,128)(2,1)S(1)} %get-tuple-element.12, bf16[32,32,256]{2,1,0:T(8,128)(2,1)S(1)} %all-to-all-done.4, bf16[32,256,256]{2,1,0:T(8,128)(2,1)} %bitcast.133), kind=kOutput, calls=%fused_computation.54 | convolution fusion | flops 134234112 | bytes 4751360 | tf_op jit(solution)/shard_map/jwk,jkn->wn/dot_general | solution.py:130
  118.6 67.1 %all-to-all-done = bf16[32,48,1024]{2,1,0:T(8,128)(2,1)} async-done(((bf16[32,48,1024]{2,1,0:T(8,128)(2,1)}), bf16[32,48,1024]{2,1,0:T(8,128)(2,1)}, u32[]{:S(2)}, u32[]{:S(2)}) %all-to-all-start) | async-done | bytes 3145760 | tf_op jit(solution)/shard_map/all_to_all | solution.py:105
  186.7 8.0 %all-to-all-start.5 = ((bf16[32,32,256]{2,1,0:T(8,128)(2,1)}), bf16[32,32,256]{2,1,0:T(8,128)(2,1)S(1)}, u32[]{:S(2)}, u32[]{:S(2)}) async-start(bf16[32,32,256]{2,1,0:T(8,128)(2,1)} %broadcast_in_dim.107), calls=%async_computation.6 | async-start | bytes 1048576 | tf_op jit(solution)/shard_map/all_to_all | solution.py:12
  194.8 4.1 %fusion.36 = f32[1536,256]{1,0:T(8,128)} fusion(bf16[1536,1024]{1,0:T(8,128)(2,1)} %bitcast.16, bf16[1024,256]{1,0:T(8,128)(2,1)S(1)} %copy-done), kind=kOutput, calls=%fused_computation.66 | convolution fusion | flops 805306368 | bytes 5242880 | tf_op jit(solution)/shard_map/dot_general | solution.py:103
  198.9 13.3 %all-to-all-done.5 = bf16[32,32,256]{2,1,0:T(8,128)(2,1)S(1)} async-done(((bf16[32,32,256]{2,1,0:T(8,128)(2,1)}), bf16[32,32,256]{2,1,0:T(8,128)(2,1)S(1)}, u32[]{:S(2)}, u32[]{:S(2)}) %all-to-all-start.5) | async-done | bytes 524320 | tf_op jit(solution)/shard_map/all_to_all | solution.py:12
  212.2 3.2 %bitcast_dynamic-update-slice_fusion.1 = (bf16[5,32,256]{2,1,0:T(8,128)(2,1)S(1)}, bf16[32,256]{1,0:T(8,128)(2,1)S(1)}) fusion(bf16[5,32,256]{2,1,0:T(8,128)(2,1)S(1)} %get-tuple-element.14, bf16[32,32,256]{2,1,0:T(8,128)(2,1)S(1)} %all-to-all-done.5, bf16[32,256,256]{2,1,0:T(8,128)(2,1)} %bitcast.134), kind=kOutput, calls=%fused_computation.53 | convolution fusion | flops 134234112 | bytes 4751360 | tf_op jit(solution)/shard_map/jwk,jkn->wn/dot_general | solution.py:130
  215.5 21.5 %all_to_all.41 = bf16[32,32,256]{2,1,0:T(8,128)(2,1)S(1)} all-to-all(bf16[32,32,256]{2,1,0:T(8,128)(2,1)S(1)} %broadcast_in_dim.108), channel_id=1, replica_groups=mesh['dp'=32,'tensor'=8] {'dp'}, dimensions={0} | all-to-all | bytes 1048576 | tf_op jit(solution)/shard_map/all_to_all | solution.py:12
  238.7 4.9 %all-to-all-start.7 = ((bf16[32,32,256]{2,1,0:T(8,128)(2,1)}), bf16[32,32,256]{2,1,0:T(8,128)(2,1)S(1)}, u32[]{:S(2)}, u32[]{:S(2)}) async-start(bf16[32,32,256]{2,1,0:T(8,128)(2,1)} %broadcast_in_dim.109), calls=%async_computation.8 | async-start | bytes 1048576 | tf_op jit(solution)/shard_map/all_to_all | solution.py:12
  245.4 14.9 %all-to-all-done.7 = bf16[32,32,256]{2,1,0:T(8,128)(2,1)S(1)} async-done(((bf16[32,32,256]{2,1,0:T(8,128)(2,1)}), bf16[32,32,256]{2,1,0:T(8,128)(2,1)S(1)}, u32[]{:S(2)}, u32[]{:S(2)}) %all-to-all-start.7) | async-done | bytes 524320 | tf_op jit(solution)/shard_map/all_to_all | solution.py:12
  260.3 3.0 %fusion.22 = bf16[5,32,256]{2,1,0:T(8,128)(2,1)S(1)} fusion(bf16[5,32,256]{2,1,0:T(8,128)(2,1)S(1)} %get-tuple-element.18, bf16[32,32,256]{2,1,0:T(8,128)(2,1)S(1)} %all-to-all-done.7, bf16[32,256,256]{2,1,0:T(8,128)(2,1)} %bitcast.135), kind=kOutput, calls=%fused_computation.31 | convolution fusion | flops 134234112 | bytes 4734976 | tf_op jit(solution)/shard_map/jwk,jkn->wn/dot_general | solution.py:130
  (45 shorter events, 10.9 us)
Async XLA Ops:
  7.2 43.2 %copy-start = (bf16[1024,256]{1,0:T(8,128)(2,1)S(1)}, bf16[1024,256]{1,0:T(8,128)(2,1)}, u32[]{:S(2)}) copy-start(bf16[1024,256]{1,0:T(8,128)(2,1)} %param.18) | copy-start | bytes 1572868
  7.2 28.1 %copy-start.4 = (s32[32]{0:T(128)S(1)}, s32[32]{0:T(128)}, u32[]{:S(2)}) copy-start(s32[32]{0:T(128)} %param.16) | copy-start | bytes 388
  7.2 47.5 %copy-start.2 = (bf16[32,6,256]{2,0,1:T(8,128)(2,1)S(1)}, bf16[32,6,256]{2,0,1:T(8,128)(2,1)}, u32[]{:S(2)}) copy-start(bf16[32,6,256]{2,0,1:T(8,128)(2,1)} %param.17) | copy-start | bytes 294916
  7.2 75.7 %all-gather.2.cloned.1.call-start = ((), (), s32[]{:S(2)}) async-start(), calls=%async_computation.10 | async-start | bytes 4718592 | tf_op jit(solution)/shard_map/all_gather | solution.py:53
  7.9 6.0 %collective-permute-start = (s32[32]{0:T(128)}, s32[32]{0:T(128)S(1)}, u32[]{:S(2)}, u32[]{:S(2)}) collective-permute-start(s32[32]{0:T(128)} %param.16), channel_id=1, source_target_pairs={{0,0},{32,1},{64,2},{96,3},{128,4},{160,5},{192,6},{224,7},{8,8},{... | collective-permute-start | bytes 392 | tf_op jit(solution)/shard_map/ppermute | solution.py:23
  16.2 34.2 %all-to-all-start.1 = ((bf16[32,8,1024]{2,1,0:T(8,128)(2,1)}), bf16[32,8,1024]{2,1,0:T(8,128)(2,1)S(1)}, u32[]{:S(2)}, u32[]{:S(2)}) async-start(bf16[32,8,1024]{2,1,0:T(8,128)(2,1)} %broadcast_in_dim.104), calls=%async_computation.2 | async-start | bytes 1048576 | tf_op jit(solution)/shard_map/all_to_all | solution.py:12
  51.3 9.4 %all-to-all-start.2 = ((bf16[8,32,256]{2,1,0:T(8,128)(2,1)}), bf16[8,32,256]{2,1,0:T(8,128)(2,1)S(1)}, u32[]{:S(2)}, u32[]{:S(2)}) async-start(bf16[8,32,256]{2,1,0:T(8,128)(2,1)} %bitcast.20), calls=%async_computation.3 | async-start | bytes 262144 | tf_op jit(solution)/shard_map/all_to_all | solution.py:93
  86.8 21.8 %all-to-all-start.4 = ((bf16[32,32,256]{2,1,0:T(8,128)(2,1)}), bf16[32,32,256]{2,1,0:T(8,128)(2,1)S(1)}, u32[]{:S(2)}, u32[]{:S(2)}) async-start(bf16[32,32,256]{2,1,0:T(8,128)(2,1)} %broadcast_in_dim.106), calls=%async_computation.5 | async-start | bytes 1048576 | tf_op jit(solution)/shard_map/all_to_all | solution.py:12
  110.7 75.1 %all-to-all-start = ((bf16[32,48,1024]{2,1,0:T(8,128)(2,1)}), bf16[32,48,1024]{2,1,0:T(8,128)(2,1)}, u32[]{:S(2)}, u32[]{:S(2)}) async-start(bf16[32,48,1024]{2,1,0:T(8,128)(2,1)} %stack.21), calls=%async_computation | async-start | bytes 6291456 | tf_op jit(solution)/shard_map/all_to_all | solution.py:105
  186.7 25.5 %all-to-all-start.5 = ((bf16[32,32,256]{2,1,0:T(8,128)(2,1)}), bf16[32,32,256]{2,1,0:T(8,128)(2,1)S(1)}, u32[]{:S(2)}, u32[]{:S(2)}) async-start(bf16[32,32,256]{2,1,0:T(8,128)(2,1)} %broadcast_in_dim.107), calls=%async_computation.6 | async-start | bytes 1048576 | tf_op jit(solution)/shard_map/all_to_all | solution.py:12
  194.7 49.0 %reduce-scatter.2.cloned.1.call-start = ((), (), s32[]{:S(2)}) async-start(), calls=%async_computation.9 | async-start | bytes 1769472 | tf_op jit(solution)/shard_map/reduce_scatter | solution.py:119
  212.2 24.8 %copy-start.1 = (bf16[8192,256]{1,0:T(8,128)(2,1)S(1)}, bf16[8192,256]{1,0:T(8,128)(2,1)}, u32[]{:S(2)}) copy-start(bf16[8192,256]{1,0:T(8,128)(2,1)} %all-gather.2.cloned.1.call-done) | copy-start | bytes 12582916
  238.7 21.6 %all-to-all-start.7 = ((bf16[32,32,256]{2,1,0:T(8,128)(2,1)}), bf16[32,32,256]{2,1,0:T(8,128)(2,1)S(1)}, u32[]{:S(2)}, u32[]{:S(2)}) async-start(bf16[32,32,256]{2,1,0:T(8,128)(2,1)} %broadcast_in_dim.109), calls=%async_computation.8 | async-start | bytes 1048576 | tf_op jit(solution)/shard_map/all_to_all | solution.py:12
  263.3 0.6 copy-start.3
Sparse Core Ops, SparseCore 0:
  9.9 37.2 all-gather.1
  199.1 34.5 reduce-scatter.1
